TPU v7x, 512 devices: a whole 4x4x16 slice. The times are simulated.
512 devices in a mesh: tm: 32 (over y, z_lo), lon: 16 (over x, z_hi, core).
Axes of the slice: x: 4, y: 4, z: 16 (z_hi: 2, z_lo: 8; z = z_hi * 8 + z_lo), core: 2. Of those that a mesh axis runs over, the one named last changes fastest.
Arguments:
- field: bfloat16 [4096, 288, 512], P('tm', 'lon'), may hold values from -15 to 15
- omega: bfloat16 [288, 512, 64], P('lon'), may hold values from -0.015625 to 0.015625
Outputs:
- projected: bfloat16 [4096, 288, 512], P('tm', 'lon')
- series: float32 [4096, 64], P('tm')
All inputs are finite; a program needn't handle non-finite values.
Results may differ from a plain program's by a relative error of at most 0.0082.
Values may be sent and summed in bfloat16 or wider, within the bound.
A program may use at most 64 MiB of HBM per device.

v0:
```python
import math
import jax
import jax.numpy as jnp
from jax import lax
from jax.sharding import PartitionSpec as P

NLAT = 32
NVAR = 16
HALF = 15
RANK = 64


def with_halo(block, sides, width, periodic):
    for axis, dim in sides:
        count = lax.axis_size(axis)
        forward = [(i, i + 1) for i in range(count - 1)]
        if periodic:
            forward.append((count - 1, 0))
        backward = [(target, source) for source, target in forward]
        low = lax.ppermute(
            lax.slice_in_dim(block, block.shape[dim] - width, None, axis=dim), axis, forward
        )
        high = lax.ppermute(lax.slice_in_dim(block, 0, width, axis=dim), axis, backward)
        block = jnp.concatenate([low, block, high], axis=dim)
    return block


def band_taps(half):
    offsets = jnp.arange(-half, half + 1).astype(jnp.float32)
    safe = jnp.where(offsets == 0, 1.0, offsets)
    core = (jnp.sin(2.0 * math.pi * safe / 3.0) - jnp.sin(2.0 * math.pi * safe / 30.0)) / (
        math.pi * safe
    )
    core = jnp.where(offsets == 0, 2.0 * (1.0 / 3.0 - 1.0 / 30.0), core)
    spread = math.pi * safe / (half + 1)
    sigma = jnp.where(offsets == 0, 1.0, jnp.sin(spread) / spread)
    return (core * sigma).astype(jnp.bfloat16)


def local(field, omega):
    days, lon_dev, cols = field.shape
    width = lon_dev * cols
    extended = with_halo(field, (("tm", 0),), HALF, False)
    extended = with_halo(extended, (("lon", 1),), 1, True)
    taps = band_taps(HALF).astype(jnp.float32)
    row_index = lax.broadcasted_iota(jnp.int32, (days, days + 2 * HALF), 0)
    col_index = lax.broadcasted_iota(jnp.int32, (days, days + 2 * HALF), 1)
    offset = col_index - row_index
    tap_index = jnp.arange(2 * HALF + 1, dtype=jnp.int32)
    toeplitz = jnp.sum(jnp.where(offset[:, :, None] == tap_index, taps, 0.0), axis=-1).astype(
        jnp.bfloat16
    )
    filtered = jnp.einsum("ij,jlc->ilc", toeplitz, extended, preferred_element_type=jnp.float32)
    across = filtered[:, :-2] + 2.0 * filtered[:, 1:-1] + filtered[:, 2:]
    grid = across.reshape(days, lon_dev, NVAR, NLAT)
    lat_pad = jnp.pad(grid, ((0, 0), (0, 0), (0, 0), (1, 1)))
    smooth = (lat_pad[..., :-2] + 2.0 * lat_pad[..., 1:-1] + lat_pad[..., 2:]) * 0.0625
    anomalies = smooth.reshape(days, width).astype(jnp.bfloat16)
    flat_omega = omega.reshape(width, RANK)
    partial_sketch = jnp.dot(anomalies, flat_omega, preferred_element_type=jnp.float32)
    sketch = lax.psum(partial_sketch, "lon")
    local_gram = jnp.dot(sketch.T, sketch, precision=lax.Precision.HIGHEST)
    gram = lax.psum(local_gram, "tm")
    lower = jnp.linalg.cholesky(gram)
    basis = jax.scipy.linalg.solve_triangular(lower, sketch.T, lower=True).T
    series = basis * math.sqrt(days * lax.axis_size("tm"))
    basis_b = basis.astype(jnp.bfloat16)
    terms = jnp.einsum("ts,tk->sk", anomalies, basis_b, preferred_element_type=jnp.float32)
    patterns = lax.psum(terms, "tm").astype(jnp.bfloat16)
    projected = jnp.einsum(
        "tk,sk->ts", basis_b, patterns, preferred_element_type=jnp.float32
    ).astype(jnp.bfloat16)
    return (projected.reshape(days, lon_dev, cols), series)


def solution(mesh):
    in_specs = (P("tm", "lon", None), P("lon", None, None))
    out_specs = (P("tm", "lon", None), P("tm", None))
    return jax.shard_map(local, mesh=mesh, in_specs=in_specs, out_specs=out_specs, check_vma=False)
```

profile of v0, /device:TPU:4, one launch (start us, length us, event | category | flops | bytes accessed | tf_op | source)
XLA Modules:
  0.0 712.1 jit_solution(13577348520286733900)
XLA Ops:
  0.6 1.3 fusion.27
  1.9 3.8 collective-permute-start
  5.8 1.3 collective-permute-start.1
  7.1 1.4 copy.20
  8.6 3.5 collective-permute-done
  12.0 10.3 %collective-permute-done.1 = bf16[15,18,512]{2,0,1:T(8,128)(2,1)S(1)} collective-permute-done((bf16[15,18,512]{2,0,1:T(8,128)(2,1)S(1)}, bf16[15,18,512]{2,0,1:T(8,128)(2,1)S(1)}, u32[]{:S(2)}, u32[]{:S(2)}) %collective-permute-start.1) | collective-permute-done | bytes 276512 | tf_op jit(solution)/shard_map/ppermute | solution.py:23
  22.4 1.9 collective-permute-start.2
  24.3 13.3 %collective-permute-start.3 = (bf16[158,1,512]{2,0,1:T(8,128)(2,1)S(1)}, bf16[158,1,512]{2,0,1:T(8,128)(2,1)S(1)}, u32[]{:S(2)}, u32[]{:S(2)}) collective-permute-start(bf16[158,1,512]{2,0,1:T(8,128)(2,1)S(1)} %get-tuple-element.9), channel_id=1, source_target_pairs={{1,0},{2,1},{3,2},{4,3},{5,4},{6,5},{7,6},{8,7},{9,8},{10,9},{11,1... | collective-permute-start | bytes 485384 | tf_op jit(solution)/shard_map/ppermute | solution.py:23
  37.9 0.9 collective-permute-done.2
  38.8 6.9 collective-permute-done.3
  45.7 1.0 fusion.5
  46.6 2.8 slice_add_fusion
  49.5 6.1 copy.13
  55.6 6.7 fusion.3
  62.3 1.2 fusion.29
  63.5 125.3 %psum.21 = f32[128,64]{0,1:T(8,128)S(1)} all-reduce(f32[128,64]{0,1:T(8,128)} %fusion.29), channel_id=1, replica_groups=mesh['tm'=32,'lon'=16] {'lon'}, use_global_device_ids=true, to_apply=%region_1.2 | all-reduce | flops 8192 | bytes 65536 | tf_op jit(solution)/shard_map/psum | solution.py:61
  188.9 231.2 %psum.22 = f32[64,64]{0,1:T(8,128)S(1)} all-reduce(f32[64,64]{0,1:T(8,128)S(1)} %fusion.28), channel_id=1, replica_groups=mesh['tm'=32,'lon'=16] {'tm'}, use_global_device_ids=true, to_apply=%region_2.3 | all-reduce | flops 4096 | bytes 32768 | tf_op jit(solution)/shard_map/psum | solution.py:63
  420.3 5.8 cholesky.16
  427.4 4.9 custom-call.7
  432.3 0.9 broadcast_multiply_fusion
  433.2 2.3 fusion.23
  435.6 269.1 %all-reduce.2 = bf16[9216,64]{0,1:T(8,128)(2,1)S(1)} all-reduce(f32[9216,64]{0,1:T(8,128)} %fusion.23), channel_id=1, replica_groups=mesh['tm'=32,'lon'=16] {'tm'}, use_global_device_ids=true, to_apply=%region_5.6 | all-reduce | flops 589824 | bytes 3538944 | tf_op jit(solution)/shard_map/psum | solution.py:69
  705.4 2.4 copy.17
  707.9 4.3 copy.18
  (13 shorter events, 2.9 us)
Async XLA Ops:
  0.6 21.6 %copy-start = (bf16[128,18,512]{2,0,1:T(8,128)(2,1)S(1)}, bf16[128,18,512]{2,0,1:T(8,128)(2,1)}, u32[]{:S(2)}) copy-start(bf16[128,18,512]{2,0,1:T(8,128)(2,1)} %param.2) | copy-start | bytes 7077892
  1.9 10.1 %collective-permute-start = (bf16[15,18,512]{2,0,1:T(8,128)(2,1)S(1)}, bf16[15,18,512]{2,0,1:T(8,128)(2,1)S(1)}, u32[]{:S(2)}, u32[]{:S(2)}) collective-permute-start(bf16[15,18,512]{2,0,1:T(8,128)(2,1)S(1)} %get-tuple-element.10), channel_id=1, source_target_pairs={{0,16},{16,32},{32,48},{48,64},{64,80},{80,96},{96,112},{112,128},... | collective-permute-start | bytes 829448 | tf_op jit(solution)/shard_map/ppermute | solution.py:20
  5.8 16.5 %collective-permute-start.1 = (bf16[15,18,512]{2,0,1:T(8,128)(2,1)S(1)}, bf16[15,18,512]{2,0,1:T(8,128)(2,1)S(1)}, u32[]{:S(2)}, u32[]{:S(2)}) collective-permute-start(bf16[15,18,512]{2,0,1:T(8,128)(2,1)S(1)} %get-tuple-element.11), channel_id=1, source_target_pairs={{16,0},{32,16},{48,32},{64,48},{80,64},{96,80},{112,96},{128,112},... | collective-permute-start | bytes 829448 | tf_op jit(solution)/shard_map/ppermute | solution.py:23
  22.4 16.4 %collective-permute-start.2 = (bf16[158,1,512]{2,0,1:T(8,128)(2,1)S(1)}, bf16[158,1,512]{2,0,1:T(8,128)(2,1)S(1)}, u32[]{:S(2)}, u32[]{:S(2)}) collective-permute-start(bf16[158,1,512]{2,0,1:T(8,128)(2,1)S(1)} %get-tuple-element.8), channel_id=1, source_target_pairs={{0,1},{1,2},{2,3},{3,4},{4,5},{5,6},{6,7},{7,8},{8,9},{9,10},{10,1... | collective-permute-start | bytes 485384 | tf_op jit(solution)/shard_map/ppermute | solution.py:20
  24.3 21.4 %collective-permute-start.3 = (bf16[158,1,512]{2,0,1:T(8,128)(2,1)S(1)}, bf16[158,1,512]{2,0,1:T(8,128)(2,1)S(1)}, u32[]{:S(2)}, u32[]{:S(2)}) collective-permute-start(bf16[158,1,512]{2,0,1:T(8,128)(2,1)S(1)} %get-tuple-element.9), channel_id=1, source_target_pairs={{1,0},{2,1},{3,2},{4,3},{5,4},{6,5},{7,6},{8,7},{9,8},{10,9},{11,1... | collective-permute-start | bytes 485384 | tf_op jit(solution)/shard_map/ppermute | solution.py:23
where the time goes:
time: 713 us; the launch traced here: 712 us
  blocking collectives  626 us (88%)
  other arithmetic  22.1 us (3%)
  waiting for transfers between devices  21.5 us (3%)
  starting transfers between devices  20.3 us (3%)
  local copies, waits for them, and re-layouts  15.6 us (2%)
    psum x1, blocking collectives, local(): patterns = lax.psum(terms, 'tm').astype(jnp.bfloat16)  269 us
    psum x1, blocking collectives, local(): gram = lax.psum(local_gram, 'tm')  231 us
    psum x1, blocking collectives, local(): sketch = lax.psum(partial_sketch, 'lon')  125 us
    ppermute x2, waiting for transfers between devices, with_halo(): lax.ppermute(lax.slice_in_dim(block, 0, width, axis=dim), axis, backward)  17.2 us
    ppermute x2, starting transfers between devices, with_halo(): lax.ppermute(lax.slice_in_dim(block, 0, width, axis=dim), axis, backward)  14.5 us
  transfers between devices with their start and end apart: 4, of which 4 were waited for; matrix products, arithmetic and copies ran while one was open for 0% of the time, Pallas kernels for 0%

commit v1 on v0

--- a/solution.py
+++ b/solution.py
@@ -58,7 +58,8 @@
     anomalies = smooth.reshape(days, width).astype(jnp.bfloat16)
     flat_omega = omega.reshape(width, RANK)
     partial_sketch = jnp.dot(anomalies, flat_omega, preferred_element_type=jnp.float32)
-    sketch = lax.psum(partial_sketch, "lon")
+    drive_task = lambda my_tile, a_name: lax.all_gather(my_tile, a_name).sum(axis=0)
+    sketch = drive_task(partial_sketch, "lon")
     local_gram = jnp.dot(sketch.T, sketch, precision=lax.Precision.HIGHEST)
     gram = lax.psum(local_gram, "tm")
     lower = jnp.linalg.cholesky(gram)

time: 713 us -> 636 us (0.89)
  the two profiles are of different devices: /device:TPU:4 before, /device:TPU:6 now
where the time goes in v1:
time: 636 us; the launch traced here: 635 us
  blocking collectives  550 us (86%)
  other arithmetic  22.2 us (3%)
  waiting for transfers between devices  20.8 us (3%)
  starting transfers between devices  20.3 us (3%)
  local copies, waits for them, and re-layouts  15.7 us (2%)
    psum x1, blocking collectives, local(): patterns = lax.psum(terms, 'tm').astype(jnp.bfloat16)  268 us
    psum x1, blocking collectives, local(): gram = lax.psum(local_gram, 'tm')  225 us
    all_gather x1, blocking collectives, local(): lax.all_gather(my_tile, a_name).sum(axis=0)  56.5 us
    ppermute x2, waiting for transfers between devices, with_halo(): lax.ppermute(lax.slice_in_dim(block, 0, width, axis=dim), axis, backward)  16.4 us
    ppermute x2, starting transfers between devices, with_halo(): lax.ppermute(lax.slice_in_dim(block, 0, width, axis=dim), axis, backward)  14.5 us
  transfers between devices with their start and end apart: 4, of which 4 were waited for; matrix products, arithmetic and copies ran while one was open for 0% of the time, Pallas kernels for 0%

profile of v1, /device:TPU:6, one launch (start us, length us, event | category | flops | bytes accessed | tf_op | source)
XLA Modules:
  0.0 635.1 jit_solution(10738277777765853522)
XLA Ops:
  0.6 1.3 fusion.27
  1.9 3.8 collective-permute-start
  5.8 1.3 collective-permute-start.1
  7.1 1.4 copy.26
  8.6 3.5 collective-permute-done
  12.0 10.3 %collective-permute-done.1 = bf16[15,18,512]{2,0,1:T(8,128)(2,1)S(1)} collective-permute-done((bf16[15,18,512]{2,0,1:T(8,128)(2,1)S(1)}, bf16[15,18,512]{2,0,1:T(8,128)(2,1)S(1)}, u32[]{:S(2)}, u32[]{:S(2)}) %collective-permute-start.1) | collective-permute-done | bytes 276512 | tf_op jit(solution)/shard_map/ppermute | solution.py:23
  22.4 1.9 collective-permute-start.2
  24.3 13.3 %collective-permute-start.3 = (bf16[158,1,512]{2,0,1:T(8,128)(2,1)S(1)}, bf16[158,1,512]{2,0,1:T(8,128)(2,1)S(1)}, u32[]{:S(2)}, u32[]{:S(2)}) collective-permute-start(bf16[158,1,512]{2,0,1:T(8,128)(2,1)S(1)} %get-tuple-element.11), channel_id=1, source_target_pairs={{1,0},{2,1},{3,2},{4,3},{5,4},{6,5},{7,6},{8,7},{9,8},{10,9},{11,1... | collective-permute-start | bytes 485384 | tf_op jit(solution)/shard_map/ppermute | solution.py:23
  37.9 0.9 collective-permute-done.2
  38.8 6.2 collective-permute-done.3
  44.9 1.0 fusion.5
  45.9 2.8 slice_add_fusion
  48.7 6.1 copy.19
  54.8 6.7 %fusion.3 = bf16[128,18,16,32]{0,3,2,1:T(8,128)(2,1)S(1)} fusion(f32[128,18,16,32]{0,3,2,1:T(8,128)} %bitcast.35), kind=kLoop, calls=%fused_computation.6 | loop fusion | flops 5898240 | bytes 7077888 | tf_op jit(solution)/shard_map/convert_element_type | solution.py:58
  62.1 56.5 %all-gather = f32[2048,64]{0,1:T(8,128)S(1)} all-gather(f32[128,64]{0,1:T(8,128)S(1)} %fusion.29), channel_id=2, replica_groups=mesh['tm'=32,'lon'=16] {'lon'}, dimensions={0}, use_global_device_ids=true | all-gather | bytes 557056 | tf_op jit(solution)/shard_map/all_gather | solution.py:61
  119.0 225.1 %psum.14 = f32[64,64]{0,1:T(8,128)S(1)} all-reduce(f32[64,64]{0,1:T(8,128)S(1)} %fusion.28), channel_id=1, replica_groups=mesh['tm'=32,'lon'=16] {'tm'}, use_global_device_ids=true, to_apply=%region_2.3 | all-reduce | flops 4096 | bytes 32768 | tf_op jit(solution)/shard_map/psum | solution.py:64
  344.2 5.8 cholesky.16
  351.3 4.9 custom-call.7
  356.2 0.9 broadcast_multiply_fusion
  357.1 2.3 fusion.23
  359.4 268.1 %all-reduce.2 = bf16[9216,64]{0,1:T(8,128)(2,1)S(1)} all-reduce(f32[9216,64]{0,1:T(8,128)} %fusion.23), channel_id=1, replica_groups=mesh['tm'=32,'lon'=16] {'tm'}, use_global_device_ids=true, to_apply=%region_5.6 | all-reduce | flops 589824 | bytes 3538944 | tf_op jit(solution)/shard_map/psum | solution.py:70
  627.6 0.8 convolution_convert_fusion
  628.4 2.4 copy.23
  630.8 4.3 copy.24
  (15 shorter events, 2.8 us)
Async XLA Ops:
  0.6 21.6 %copy-start = (bf16[128,18,512]{2,0,1:T(8,128)(2,1)S(1)}, bf16[128,18,512]{2,0,1:T(8,128)(2,1)}, u32[]{:S(2)}) copy-start(bf16[128,18,512]{2,0,1:T(8,128)(2,1)} %param.2) | copy-start | bytes 7077892
  1.9 10.1 %collective-permute-start = (bf16[15,18,512]{2,0,1:T(8,128)(2,1)S(1)}, bf16[15,18,512]{2,0,1:T(8,128)(2,1)S(1)}, u32[]{:S(2)}, u32[]{:S(2)}) collective-permute-start(bf16[15,18,512]{2,0,1:T(8,128)(2,1)S(1)} %get-tuple-element.12), channel_id=1, source_target_pairs={{0,16},{16,32},{32,48},{48,64},{64,80},{80,96},{96,112},{112,128},... | collective-permute-start | bytes 829448 | tf_op jit(solution)/shard_map/ppermute | solution.py:20
  5.8 16.5 %collective-permute-start.1 = (bf16[15,18,512]{2,0,1:T(8,128)(2,1)S(1)}, bf16[15,18,512]{2,0,1:T(8,128)(2,1)S(1)}, u32[]{:S(2)}, u32[]{:S(2)}) collective-permute-start(bf16[15,18,512]{2,0,1:T(8,128)(2,1)S(1)} %get-tuple-element.13), channel_id=1, source_target_pairs={{16,0},{32,16},{48,32},{64,48},{80,64},{96,80},{112,96},{128,112},... | collective-permute-start | bytes 829448 | tf_op jit(solution)/shard_map/ppermute | solution.py:23
  22.4 16.4 %collective-permute-start.2 = (bf16[158,1,512]{2,0,1:T(8,128)(2,1)S(1)}, bf16[158,1,512]{2,0,1:T(8,128)(2,1)S(1)}, u32[]{:S(2)}, u32[]{:S(2)}) collective-permute-start(bf16[158,1,512]{2,0,1:T(8,128)(2,1)S(1)} %get-tuple-element.10), channel_id=1, source_target_pairs={{0,1},{1,2},{2,3},{3,4},{4,5},{5,6},{6,7},{7,8},{8,9},{9,10},{10,1... | collective-permute-start | bytes 485384 | tf_op jit(solution)/shard_map/ppermute | solution.py:20
  24.3 20.6 %collective-permute-start.3 = (bf16[158,1,512]{2,0,1:T(8,128)(2,1)S(1)}, bf16[158,1,512]{2,0,1:T(8,128)(2,1)S(1)}, u32[]{:S(2)}, u32[]{:S(2)}) collective-permute-start(bf16[158,1,512]{2,0,1:T(8,128)(2,1)S(1)} %get-tuple-element.11), channel_id=1, source_target_pairs={{1,0},{2,1},{3,2},{4,3},{5,4},{6,5},{7,6},{8,7},{9,8},{10,9},{11,1... | collective-permute-start | bytes 485384 | tf_op jit(solution)/shard_map/ppermute | solution.py:23
